TPU v7x, 256 devices: a whole 4x4x8 slice. The times are simulated.
256 devices in a mesh: wide: 32 (over z, y), narrow: 8 (over x, core).
Axes of the slice: x: 4, y: 4, z: 8, core: 2. Of those that a mesh axis runs over, the one named last changes fastest.
Arguments:
- upstream_hot: bfloat16 [524288, 512], P(('wide', 'narrow')), may hold values from -6 to 6
- upstream_warm: bfloat16 [524288, 512], P(('wide', 'narrow')), may hold values from -6 to 6
- upstream_cold: bfloat16 [524288, 512], P(('wide', 'narrow')), may hold values from -6 to 6
- saved_hot: bfloat16 [524288, 512], P(('wide', 'narrow')), may hold values from -6 to 6
- saved_warm: bfloat16 [524288, 128], P(('wide', 'narrow')), may hold values from -6 to 6
- saved_cold: bfloat16 [32, 524288], P(None, ('wide', 'narrow')), may hold values from -6 to 6
- weight_hot: bfloat16 [512, 512], replicated, may hold values from -0.25 to 0.25
- weight_warm: bfloat16 [128, 512], replicated, may hold values from -0.25 to 0.25
- weight_cold: bfloat16 [32, 512], replicated, may hold values from -0.25 to 0.25
- owner_hot: int32 [524288, 1], P(('wide', 'narrow')), may hold values from 0 to 255; in each aligned block of 2048 rows (0 to 2047, 2048 to 4095, ...) at most 16 rows name the same one
- owner_warm: int32 [524288, 1], P(('wide', 'narrow')), may hold values from 0 to 255; in each aligned block of 2048 rows (0 to 2047, 2048 to 4095, ...) at most 16 rows name the same one
- owner_cold: int32 [524288, 1], P(('wide', 'narrow')), may hold values from 0 to 255; in each aligned block of 2048 rows (0 to 2047, 2048 to 4095, ...) at most 16 rows name the same one
- local_hot: int32 [524288], P(('wide', 'narrow')), may hold values from 0 to 511
- local_warm: int32 [524288], P(('wide', 'narrow')), may hold values from 0 to 2047
- local_cold: int32 [524288], P(('wide', 'narrow')), may hold values from 0 to 4095
Outputs:
- table_hot: float32 [131072, 512], P(('wide', 'narrow'))
- table_warm: float32 [524288, 128], P(('wide', 'narrow'))
- table_cold: float32 [32, 1048576], P(None, ('wide', 'narrow'))
- mixing_hot: float32 [512, 512], replicated
- mixing_warm: float32 [128, 512], replicated
- mixing_cold: float32 [32, 512], replicated
Inputs may be any that keep to these rules, and one draw needn't show every extreme that they name: `owner_hot`: among the 2048 lookups of the most frequent bucket on one device, at most 16 have the same owner, and that many is reached. `owner_warm`: among the 2048 lookups of the middle bucket on one device, at most 16 have the same owner, and that many is reached. `owner_cold`: among the 2048 lookups of the rarest bucket on one device, at most 16 have the same owner, and that many is reached.
All inputs are finite; a program needn't handle non-finite values.
Results may differ from a plain program's by a relative error of at most 0.0029.
Values may be sent and summed in bfloat16 or wider, within the bound.
A program may use at most 128 MiB of HBM per device.

v0:
```python
import math
import jax
import jax.numpy as jnp
from jax import lax
from jax.sharding import PartitionSpec as P

W_HOT = 512
W_WARM = 128
W_COLD = 32
LOOK = 2048
ROWS_HOT = 512
ROWS_WARM = 2048
ROWS_COLD = 4096


def project(values, weight):
    return lax.dot_general(
        values, weight, (((1,), (1,)), ((), ())), preferred_element_type=jnp.float32
    )


def pack_rows(values, owners, local_rows, capacity, devices, narrow_size):
    targets = lax.iota(jnp.int32, devices)
    onehot = (owners[:, None] == targets[None, :]).astype(jnp.int32)
    position = jnp.sum(jnp.cumsum(onehot, axis=0) * onehot, axis=1) - 1
    placed = owners * capacity + position
    columns = values.shape[1]
    buffer = jnp.zeros((devices * capacity, columns), values.dtype).at[placed].set(values)
    labels = jnp.full((devices * capacity,), -1, jnp.int32).at[placed].set(local_rows)
    wide_size = devices // narrow_size
    return (
        buffer.reshape(wide_size, narrow_size, capacity * columns),
        labels.reshape(wide_size, narrow_size, capacity),
    )


def segment_rows(terms, labels, table_rows, transposed):
    block_rows = min(512, table_rows)
    flat_labels = labels.reshape(-1)

    def one_block(start):
        index_rows = start + lax.iota(jnp.int32, block_rows)
        if transposed:
            onehot = (flat_labels[:, None] == index_rows[None, :]).astype(jnp.bfloat16)
            return lax.dot_general(
                terms, onehot, (((0,), (0,)), ((), ())), preferred_element_type=jnp.float32
            )
        onehot = (index_rows[:, None] == flat_labels[None, :]).astype(jnp.bfloat16)
        return jnp.dot(onehot, terms, preferred_element_type=jnp.float32)

    starts = jnp.arange(table_rows // block_rows, dtype=jnp.int32) * block_rows
    blocks = lax.map(one_block, starts)
    if transposed:
        return jnp.transpose(blocks, (1, 0, 2)).reshape(terms.shape[1], table_rows)
    return blocks.reshape(table_rows, terms.shape[1])


def per_device(
    upstream_hot,
    upstream_warm,
    upstream_cold,
    saved_hot,
    saved_warm,
    saved_cold,
    weight_hot,
    weight_warm,
    weight_cold,
    owner_hot,
    owner_warm,
    owner_cold,
    local_hot,
    local_warm,
    local_cold,
):
    narrow_size = lax.axis_size("narrow")
    devices = lax.axis_size("wide") * narrow_size
    capacity = max(2, 2 * LOOK // devices)
    sent_hot, label_hot = pack_rows(
        project(upstream_hot, weight_hot).astype(jnp.bfloat16),
        owner_hot[:, 0],
        local_hot,
        capacity,
        devices,
        narrow_size,
    )
    sent_warm, label_warm = pack_rows(
        project(upstream_warm, weight_warm).astype(jnp.bfloat16),
        owner_warm[:, 0],
        local_warm,
        capacity,
        devices,
        narrow_size,
    )
    sent_cold, label_cold = pack_rows(
        project(upstream_cold, weight_cold).astype(jnp.bfloat16),
        owner_cold[:, 0],
        local_cold,
        capacity,
        devices,
        narrow_size,
    )
    got_hot, got_warm, got_cold, lab_hot, lab_warm, lab_cold = (
        lax.all_to_all(
            lax.all_to_all(sent_hot, "wide", split_axis=0, concat_axis=0, tiled=True),
            "narrow",
            split_axis=1,
            concat_axis=1,
            tiled=True,
        ),
        lax.all_to_all(
            lax.all_to_all(sent_warm, "wide", split_axis=0, concat_axis=0, tiled=True),
            "narrow",
            split_axis=1,
            concat_axis=1,
            tiled=True,
        ),
        lax.all_to_all(
            lax.all_to_all(sent_cold, "wide", split_axis=0, concat_axis=0, tiled=True),
            "narrow",
            split_axis=1,
            concat_axis=1,
            tiled=True,
        ),
        lax.all_to_all(
            lax.all_to_all(label_hot, "wide", split_axis=0, concat_axis=0, tiled=True),
            "narrow",
            split_axis=1,
            concat_axis=1,
            tiled=True,
        ),
        lax.all_to_all(
            lax.all_to_all(label_warm, "wide", split_axis=0, concat_axis=0, tiled=True),
            "narrow",
            split_axis=1,
            concat_axis=1,
            tiled=True,
        ),
        lax.all_to_all(
            lax.all_to_all(label_cold, "wide", split_axis=0, concat_axis=0, tiled=True),
            "narrow",
            split_axis=1,
            concat_axis=1,
            tiled=True,
        ),
    )
    term_hot = got_hot.reshape(-1, W_HOT)
    term_warm = got_warm.reshape(-1, W_WARM)
    term_cold = got_cold.reshape(-1, W_COLD)
    table_hot = segment_rows(term_hot, lab_hot, ROWS_HOT, False)
    table_warm = segment_rows(term_warm, lab_warm, ROWS_WARM, False)
    table_cold = segment_rows(term_cold, lab_cold, ROWS_COLD, True)
    part_hot = lax.dot_general(
        saved_hot, upstream_hot, (((0,), (0,)), ((), ())), preferred_element_type=jnp.float32
    )
    part_warm = lax.dot_general(
        saved_warm, upstream_warm, (((0,), (0,)), ((), ())), preferred_element_type=jnp.float32
    )
    part_cold = jnp.dot(saved_cold, upstream_cold, preferred_element_type=jnp.float32)
    factor = 1.0 / math.sqrt(LOOK * devices)
    total_hot, total_warm, total_cold = lax.psum(
        (part_hot, part_warm, part_cold), ("wide", "narrow")
    )
    return (
        table_hot,
        table_warm,
        table_cold,
        total_hot * factor,
        total_warm * factor,
        total_cold * factor,
    )


def solution(mesh):
    placed = (
        P(("wide", "narrow"), None),
        P(("wide", "narrow"), None),
        P(("wide", "narrow"), None),
        P(("wide", "narrow"), None),
        P(("wide", "narrow"), None),
        P(None, ("wide", "narrow")),
        P(),
        P(),
        P(),
        P(("wide", "narrow"), None),
        P(("wide", "narrow"), None),
        P(("wide", "narrow"), None),
        P(("wide", "narrow")),
        P(("wide", "narrow")),
        P(("wide", "narrow")),
    )
    return jax.shard_map(
        per_device,
        mesh=mesh,
        in_specs=placed,
        out_specs=(
            P(("wide", "narrow"), None),
            P(("wide", "narrow"), None),
            P(None, ("wide", "narrow")),
            P(),
            P(),
            P(),
        ),
        check_vma=False,
    )
```

profile of v0, /device:TPU:1, one launch (start us, length us, event | category | flops | bytes accessed | tf_op | source)
XLA Modules:
  0.0 585.1 jit_solution(10837068983426819529)
XLA Ops:
  8.5 1.3 copy-done.2
  9.9 1.8 broadcast_add_fusion.2
  11.7 1.2 copy.50
  14.5 8.2 %scatter_custom_fusion = s32[4096]{0:T(1024)S(1)} fusion(s32[2048]{0:T(1024)S(1)} %bitcast.108, s32[2048]{0:T(1024)} %param.31, s32[]{:T(128)} %constant.28.clone.1), kind=kCustom, calls=%fused_computation.69 | custom fusion | bytes 16896 | tf_op jit(solution)/shard_map/scatter | solution.py:29
  23.5 12.0 %all-to-all-start = ((s32[32,1,128]{2,1,0:T(1,128)}), s32[32,1,128]{2,1,0:T(1,128)S(1)}, u32[]{:S(2)}, u32[]{:S(2)}) async-start(s32[32,1,128]{2,1,0:T(1,128)} %reshape.208), calls=%async_computation | async-start | bytes 32768 | tf_op jit(solution)/shard_map/all_to_all | solution.py:125
  36.0 1.3 copy-done.3
  37.4 1.8 broadcast_add_fusion.1
  41.9 1.3 copy-done.4
  43.3 1.8 broadcast_add_fusion
  47.3 8.2 %scatter_custom_fusion.2 = s32[4096]{0:T(1024)S(1)} fusion(s32[2048]{0:T(1024)S(1)} %bitcast.110, s32[2048]{0:T(1024)} %param.32, s32[]{:T(128)} %constant.28.clone.1), kind=kCustom, calls=%fused_computation.67 | custom fusion | bytes 16896 | tf_op jit(solution)/shard_map/scatter | solution.py:29
  56.3 9.2 %all-to-all-start.4 = ((s32[32,1,128]{2,1,0:T(1,128)}), s32[32,1,128]{2,1,0:T(1,128)S(1)}, u32[]{:S(2)}, u32[]{:S(2)}) async-start(s32[32,1,128]{2,1,0:T(1,128)} %reshape.212), calls=%async_computation.4 | async-start | bytes 32768 | tf_op jit(solution)/shard_map/all_to_all | solution.py:132
  65.6 8.2 %scatter_custom_fusion.4 = s32[4096]{0:T(1024)S(1)} fusion(s32[2048]{0:T(1024)S(1)} %bitcast.112, s32[2048]{0:T(1024)} %param.33, s32[]{:T(128)} %constant.28.clone.1), kind=kCustom, calls=%fused_computation.65 | custom fusion | bytes 16896 | tf_op jit(solution)/shard_map/scatter | solution.py:29
  74.6 9.2 %all-to-all-start.8 = ((s32[32,1,128]{2,1,0:T(1,128)}), s32[32,1,128]{2,1,0:T(1,128)S(1)}, u32[]{:S(2)}, u32[]{:S(2)}) async-start(s32[32,1,128]{2,1,0:T(1,128)} %reshape.216), calls=%async_computation.8 | async-start | bytes 32768 | tf_op jit(solution)/shard_map/all_to_all | solution.py:139
  86.0 6.4 %all-to-all-done.8 = s32[32,1,128]{2,1,0:T(1,128)S(1)} async-done(((s32[32,1,128]{2,1,0:T(1,128)}), s32[32,1,128]{2,1,0:T(1,128)S(1)}, u32[]{:S(2)}, u32[]{:S(2)}) %all-to-all-start.8) | async-done | bytes 16416 | tf_op jit(solution)/shard_map/all_to_all | solution.py:139
  92.4 7.5 %all-to-all-start.1 = ((s32[8,1,512]{2,1,0:T(1,128)}), s32[8,1,512]{2,1,0:T(1,128)S(1)}, u32[]{:S(2)}, u32[]{:S(2)}) async-start(s32[8,1,512]{2,1,0:T(1,128)} %reshape.210), calls=%async_computation.1 | async-start | bytes 32768 | tf_op jit(solution)/shard_map/all_to_all | solution.py:124
  101.5 3.1 all-to-all-done.1
  104.6 3.9 all-to-all-start.5
  108.5 2.3 convolution_convert_fusion.2
  111.9 6.4 %scatter_custom_fusion.5 = bf16[4096,32]{1,0:T(8,128)(2,1)S(1)} fusion(s32[2048]{0:T(1024)S(1)} %bitcast.113, bf16[2048,32]{1,0:T(8,128)(2,1)} %copy.64, bf16[]{:T(256)} %constant.37.clone.1), kind=kCustom, calls=%fused_computation.53 | custom fusion | bytes 262656 | tf_op jit(solution)/shard_map/scatter | solution.py:28
  118.3 1.7 reshape.145
  120.0 3.9 all-to-all-start.10
  125.4 10.5 %all-to-all-done.10 = bf16[32,8,512]{2,1,0:T(8,128)(2,1)S(1)} async-done(((bf16[32,8,512]{2,1,0:T(8,128)(2,1)}), bf16[32,8,512]{2,1,0:T(8,128)(2,1)S(1)}, u32[]{:S(2)}, u32[]{:S(2)}) %all-to-all-start.10) | async-done | bytes 262176 | tf_op jit(solution)/shard_map/all_to_all | solution.py:118
  136.0 6.2 %all-to-all-start.9 = ((s32[8,1,512]{2,1,0:T(1,128)}), s32[8,1,512]{2,1,0:T(1,128)S(1)}, u32[]{:S(2)}, u32[]{:S(2)}) async-start(s32[8,1,512]{2,1,0:T(1,128)} %reshape.218), calls=%async_computation.9 | async-start | bytes 32768 | tf_op jit(solution)/shard_map/all_to_all | solution.py:138
  143.0 3.9 all-to-all-done.9
  147.4 4.0 all-to-all-start.11
  151.5 3.1 convolution_convert_fusion.1
  154.6 6.4 %scatter_custom_fusion.3 = bf16[4096,128]{1,0:T(8,128)(2,1)S(1)} fusion(s32[2048]{0:T(1024)} %bitcast.111, bf16[2048,128]{1,0:T(8,128)(2,1)} %convolution_convert_fusion.1, bf16[]{:T(256)} %constant.37.clone.1), kind=kCustom, calls=%fused_computation.55 | custom fusion | bytes 1049088 | tf_op jit(solution)/shard_map/scatter | solution.py:28
  161.0 1.3 reshape.140
  162.2 4.1 all-to-all-start.6
  166.4 3.7 convolution_convert_fusion
  170.0 12.6 %scatter_custom_fusion.1 = bf16[4096,512]{1,0:T(8,128)(2,1)} fusion(s32[2048]{0:T(1024)} %bitcast.109, bf16[2048,512]{1,0:T(8,128)(2,1)} %convolution_convert_fusion, bf16[]{:T(256)} %constant.37.clone.1), kind=kCustom, calls=%fused_computation.40 | custom fusion | bytes 4194816 | tf_op jit(solution)/shard_map/scatter | solution.py:28
  182.6 7.4 %reshape.136 = bf16[32,8,8192]{2,1,0:T(8,128)(2,1)} reshape(bf16[4096,512]{1,0:T(8,128)(2,1)} %scatter_custom_fusion.1) | data formatting | bytes 8388608 | tf_op jit(solution)/shard_map/reshape | solution.py:32
  190.0 4.4 all-to-all-done.6
  194.4 5.3 all-to-all-start.2
  199.8 2.8 fusion.48
  202.6 2.2 fusion.47
  204.9 2.2 fusion.46
  207.2 1.5 copy.58
  208.7 87.6 %all-to-all-done.2 = bf16[32,8,8192]{2,1,0:T(8,128)(2,1)} async-done(((bf16[32,8,8192]{2,1,0:T(8,128)(2,1)}), bf16[32,8,8192]{2,1,0:T(8,128)(2,1)}, u32[]{:S(2)}, u32[]{:S(2)}) %all-to-all-start.2) | async-done | bytes 4194336 | tf_op jit(solution)/shard_map/all_to_all | solution.py:104
  296.3 7.0 %all-to-all-start.7 = ((bf16[32,8,2048]{2,0,1:T(8,128)(2,1)}), bf16[32,8,2048]{2,0,1:T(8,128)(2,1)S(1)}, u32[]{:S(2)}, u32[]{:S(2)}) async-start(bf16[32,8,2048]{2,0,1:T(8,128)(2,1)} %copy.58), calls=%async_computation.7 | async-start | bytes 2097152 | tf_op jit(solution)/shard_map/all_to_all | solution.py:110
  306.3 184.4 %all-reduce.3.cloned.1.call-done = (f32[512,512]{1,0:T(8,128)}, f32[128,512]{1,0:T(8,128)}, f32[32,512]{1,0:T(8,128)}) async-done(((f32[512,512]{1,0:T(8,128)}, f32[128,512]{1,0:T(8,128)}, f32[32,512]{1,0:T(8,128)}), (f32[512,512]{1,0:T(8,128)}, f32[128,512]{1,0:T(8,128)}, f32[32,512]{1,0:T(8,128)})) %all-reduce.3.cloned.1.call-update) | async-done | bytes 1376272 | tf_op jit(solution)/shard_map/psum | solution.py:160
  490.7 1.5 broadcast_multiply_fusion.2
  492.2 1.7 broadcast_multiply_fusion.1
  493.9 2.3 broadcast_multiply_fusion
  496.9 6.5 %copy.53 = bf16[32,8,8192]{2,0,1:T(8,128)(2,1)} copy(bf16[32,8,8192]{2,1,0:T(8,128)(2,1)} %all-to-all-done.2) | data formatting | bytes 8388608 | tf_op jit(solution)/shard_map/all_to_all | solution.py:104
  503.4 6.4 %all-to-all-start.3 = ((bf16[32,8,8192]{2,0,1:T(8,128)(2,1)}), bf16[32,8,8192]{2,0,1:T(8,128)(2,1)}, u32[]{:S(2)}, u32[]{:S(2)}) async-start(bf16[32,8,8192]{2,0,1:T(8,128)(2,1)} %copy.53), calls=%async_computation.3 | async-start | bytes 8388608 | tf_op jit(solution)/shard_map/all_to_all | solution.py:103
  509.8 23.5 %while.27 = (s32[]{:T(128)}, f32[8,32,512]{2,1,0:T(8,128)S(1)}, s32[32,8,16]{2,1,0:T(8,128)}, s32[8]{0:T(128)S(1)}, bf16[4096,32]{1,0:T(8,128)(2,1)S(1)}, /*index=5*/s32[4096]{0:T(1024)S(1)}, s32[]{:T(128)}) while((s32[]{:T(128)}, f32[8,32,512]{2,1,0:T(8,128)S(1)}, s32[32,8,16]{2,1,0:T(8,128)}, s32[8]{0:T(128)S(1)}, ...), condition=%wide.wide.region_18.19_spmd, body=%wide.wide.region_17.18_spmd.sunk | while | flops 136315392 | bytes 1134697 | solution.py:52
  511.1 1.7 fusion.81
  514.0 1.7 fusion.81
  517.0 1.7 fusion.81
  519.9 1.7 fusion.81
  522.9 1.7 fusion.81
  525.8 1.7 fusion.81
  528.7 1.7 fusion.81
  531.7 1.7 fusion.81
  535.3 13.0 %while.26 = (s32[]{:T(128)}, f32[4,512,128]{2,1,0:T(8,128)}, s32[4]{0:T(128)S(1)}, s32[32,8,16]{2,1,0:T(8,128)}, bf16[4096,128]{1,0:T(8,128)(2,1)S(1)}, /*index=5*/s32[4096]{0:T(1024)S(1)}, s32[]{:T(128)}) while((s32[]{:T(128)}, f32[4,512,128]{2,1,0:T(8,128)}, s32[4]{0:T(128)S(1)}, s32[32,8,16]{2,1,0:T(8,128)}, ...), condition=%wide.wide.region_11.12_spmd, body=%wide.wide.region_10.11_spmd.sunk | while | flops 538968576 | bytes 1331305 | solution.py:52
  536.6 2.0 fusion.78
  539.8 2.0 fusion.78
  543.1 2.0 fusion.78
  546.3 2.0 fusion.78
  548.3 10.2 %all-to-all-done.3 = bf16[32,8,8192]{2,0,1:T(8,128)(2,1)} async-done(((bf16[32,8,8192]{2,0,1:T(8,128)(2,1)}), bf16[32,8,8192]{2,0,1:T(8,128)(2,1)}, u32[]{:S(2)}, u32[]{:S(2)}) %all-to-all-start.3) | async-done | bytes 4194336 | tf_op jit(solution)/shard_map/all_to_all | solution.py:103
  558.6 6.5 %copy.54 = bf16[32,8,8192]{2,1,0:T(8,128)(2,1)} copy(bf16[32,8,8192]{2,0,1:T(8,128)(2,1)} %all-to-all-done.3) | data formatting | bytes 8388608 | tf_op jit(solution)/shard_map/all_to_all | solution.py:103
  565.0 7.4 %reshape.137 = bf16[4096,512]{1,0:T(8,128)(2,1)} reshape(bf16[32,8,8192]{2,1,0:T(8,128)(2,1)} %copy.54) | data formatting | bytes 8388608 | tf_op jit(solution)/shard_map/reshape | solution.py:146
  572.4 5.6 fusion.20
  (140 shorter events, 38.7 us)
Async XLA Ops:
  7.2 159.2 %copy-start = (bf16[2048,512]{1,0:T(8,128)(2,1)S(1)}, bf16[2048,512]{1,0:T(8,128)(2,1)}, u32[]{:S(2)}) copy-start(bf16[2048,512]{1,0:T(8,128)(2,1)} %param.19) | copy-start | bytes 6291460
  8.5 1.4 copy-start.2
  11.7 1.3 copy-start.11
  12.9 22.6 %copy-start.12 = (s32[2048,1]{0,1:T(1,128)S(1)}, s32[2048,1]{0,1:T(1,128)}, u32[]{:S(2)}) copy-start(s32[2048,1]{0,1:T(1,128)} %param.29) | copy-start | bytes 24580
  13.9 0.6 copy-start.19
  23.5 32.8 %all-to-all-start = ((s32[32,1,128]{2,1,0:T(1,128)}), s32[32,1,128]{2,1,0:T(1,128)S(1)}, u32[]{:S(2)}, u32[]{:S(2)}) async-start(s32[32,1,128]{2,1,0:T(1,128)} %reshape.208), calls=%async_computation | async-start | bytes 32768 | tf_op jit(solution)/shard_map/all_to_all | solution.py:125
  36.0 1.4 copy-start.3
  40.5 1.0 copy-start.13
  41.4 5.8 copy-start.20
  41.9 1.4 copy-start.4
  46.3 62.2 %copy-start.18 = (bf16[32,512]{1,0:T(8,128)(2,1)S(1)}, bf16[32,512]{1,0:T(8,128)(2,1)}, u32[]{:S(2)}) copy-start(bf16[32,512]{1,0:T(8,128)(2,1)} %param.27) | copy-start | bytes 98308
  56.3 18.3 %all-to-all-start.4 = ((s32[32,1,128]{2,1,0:T(1,128)}), s32[32,1,128]{2,1,0:T(1,128)S(1)}, u32[]{:S(2)}, u32[]{:S(2)}) async-start(s32[32,1,128]{2,1,0:T(1,128)} %reshape.212), calls=%async_computation.4 | async-start | bytes 32768 | tf_op jit(solution)/shard_map/all_to_all | solution.py:132
  74.6 17.8 %all-to-all-start.8 = ((s32[32,1,128]{2,1,0:T(1,128)}), s32[32,1,128]{2,1,0:T(1,128)S(1)}, u32[]{:S(2)}, u32[]{:S(2)}) async-start(s32[32,1,128]{2,1,0:T(1,128)} %reshape.216), calls=%async_computation.8 | async-start | bytes 32768 | tf_op jit(solution)/shard_map/all_to_all | solution.py:139
  92.4 12.2 %all-to-all-start.1 = ((s32[8,1,512]{2,1,0:T(1,128)}), s32[8,1,512]{2,1,0:T(1,128)S(1)}, u32[]{:S(2)}, u32[]{:S(2)}) async-start(s32[8,1,512]{2,1,0:T(1,128)} %reshape.210), calls=%async_computation.1 | async-start | bytes 32768 | tf_op jit(solution)/shard_map/all_to_all | solution.py:124
  104.6 15.4 %all-to-all-start.5 = ((s32[8,1,512]{2,1,0:T(1,128)}), s32[8,1,512]{2,1,0:T(1,128)S(1)}, u32[]{:S(2)}, u32[]{:S(2)}) async-start(s32[8,1,512]{2,1,0:T(1,128)} %reshape.214), calls=%async_computation.5 | async-start | bytes 32768 | tf_op jit(solution)/shard_map/all_to_all | solution.py:131
  111.9 39.6 %copy-start.10 = (bf16[128,512]{1,0:T(8,128)(2,1)S(1)}, bf16[128,512]{1,0:T(8,128)(2,1)}, u32[]{:S(2)}) copy-start(bf16[128,512]{1,0:T(8,128)(2,1)} %param.26) | copy-start | bytes 393220
  120.0 26.9 %copy-start.14 = (s32[8,1,512]{2,1,0:T(1,128)}, s32[8,1,512]{2,1,0:T(1,128)S(1)}, u32[]{:S(2)}) copy-start(s32[8,1,512]{2,1,0:T(1,128)S(1)} %all-to-all-done.5) | copy-start | bytes 49156
  120.0 16.0 %all-to-all-start.10 = ((bf16[32,8,512]{2,1,0:T(8,128)(2,1)}), bf16[32,8,512]{2,1,0:T(8,128)(2,1)S(1)}, u32[]{:S(2)}, u32[]{:S(2)}) async-start(bf16[32,8,512]{2,1,0:T(8,128)(2,1)} %reshape.145), calls=%async_computation.10 | async-start | bytes 524288 | tf_op jit(solution)/shard_map/all_to_all | solution.py:118
  136.0 10.9 %all-to-all-start.9 = ((s32[8,1,512]{2,1,0:T(1,128)}), s32[8,1,512]{2,1,0:T(1,128)S(1)}, u32[]{:S(2)}, u32[]{:S(2)}) async-start(s32[8,1,512]{2,1,0:T(1,128)} %reshape.218), calls=%async_computation.9 | async-start | bytes 32768 | tf_op jit(solution)/shard_map/all_to_all | solution.py:138
  146.8 0.6 copy-start.16
  147.4 14.8 %all-to-all-start.11 = ((bf16[32,8,512]{2,0,1:T(8,128)(2,1)}), bf16[32,8,512]{2,0,1:T(8,128)(2,1)S(1)}, u32[]{:S(2)}, u32[]{:S(2)}) async-start(bf16[32,8,512]{2,0,1:T(8,128)(2,1)} %copy.65), calls=%async_computation.11 | async-start | bytes 524288 | tf_op jit(solution)/shard_map/all_to_all | solution.py:117
  162.2 32.2 %all-to-all-start.6 = ((bf16[32,8,2048]{2,1,0:T(8,128)(2,1)}), bf16[32,8,2048]{2,1,0:T(8,128)(2,1)S(1)}, u32[]{:S(2)}, u32[]{:S(2)}) async-start(bf16[32,8,2048]{2,1,0:T(8,128)(2,1)} %reshape.140), calls=%async_computation.6 | async-start | bytes 2097152 | tf_op jit(solution)/shard_map/all_to_all | solution.py:111
  190.0 9.8 %copy-start.9 = (bf16[32,2048]{1,0:T(8,128)(2,1)S(1)}, bf16[32,2048]{1,0:T(8,128)(2,1)}, u32[]{:S(2)}) copy-start(bf16[32,2048]{1,0:T(8,128)(2,1)} %param.24) | copy-start | bytes 393220
  194.4 101.9 %all-to-all-start.2 = ((bf16[32,8,8192]{2,1,0:T(8,128)(2,1)}), bf16[32,8,8192]{2,1,0:T(8,128)(2,1)}, u32[]{:S(2)}, u32[]{:S(2)}) async-start(bf16[32,8,8192]{2,1,0:T(8,128)(2,1)} %reshape.136), calls=%async_computation.2 | async-start | bytes 8388608 | tf_op jit(solution)/shard_map/all_to_all | solution.py:104
  199.7 291.0 %all-reduce.3.cloned.1.call-start = ((), (), s32[]{:S(2)}) async-start(), calls=%async_computation.12 | async-start | bytes 2752512 | tf_op jit(solution)/shard_map/psum | solution.py:160
  199.8 2.9 copy-start.5
  199.8 5.1 copy-start.21
  207.1 97.2 %copy-start.15 = (s32[8,1,512]{2,1,0:T(1,128)S(1)}, s32[8,1,512]{2,1,0:T(1,128)}, u32[]{:S(2)}) copy-start(s32[8,1,512]{2,1,0:T(1,128)} %copy-done.14) | copy-start | bytes 49156
  207.2 98.1 %copy-start.17 = (s32[8,1,512]{2,1,0:T(1,128)S(1)}, s32[8,1,512]{2,1,0:T(1,128)}, u32[]{:S(2)}) copy-start(s32[8,1,512]{2,1,0:T(1,128)} %copy-done.16) | copy-start | bytes 49156
  296.3 207.1 %all-to-all-start.7 = ((bf16[32,8,2048]{2,0,1:T(8,128)(2,1)}), bf16[32,8,2048]{2,0,1:T(8,128)(2,1)S(1)}, u32[]{:S(2)}, u32[]{:S(2)}) async-start(bf16[32,8,2048]{2,0,1:T(8,128)(2,1)} %copy.58), calls=%async_computation.7 | async-start | bytes 2097152 | tf_op jit(solution)/shard_map/all_to_all | solution.py:110
  305.2 191.7 %copy-start.6 = (s32[32,8,16]{2,1,0:T(8,128)}, s32[32,8,16]{2,1,0:T(8,128)S(1)}, u32[]{:S(2)}) copy-start(s32[32,8,16]{2,1,0:T(8,128)S(1)} %copy.60) | copy-start | bytes 49156
  306.2 190.7 %copy-start.7 = (s32[32,8,16]{2,1,0:T(8,128)}, s32[32,8,16]{2,1,0:T(8,128)S(1)}, u32[]{:S(2)}) copy-start(s32[32,8,16]{2,1,0:T(8,128)S(1)} %copy.67) | copy-start | bytes 49156
  503.4 6.4 %copy-start.8 = (f32[8,32,512]{2,1,0:T(8,128)S(1)}, f32[8,32,512]{2,1,0:T(8,128)}, u32[]{:S(2)}) copy-start(f32[8,32,512]{2,1,0:T(8,128)} %custom-call.1) | copy-start | bytes 1572868
  503.4 55.2 %all-to-all-start.3 = ((bf16[32,8,8192]{2,0,1:T(8,128)(2,1)}), bf16[32,8,8192]{2,0,1:T(8,128)(2,1)}, u32[]{:S(2)}, u32[]{:S(2)}) async-start(bf16[32,8,8192]{2,0,1:T(8,128)(2,1)} %copy.53), calls=%async_computation.3 | async-start | bytes 8388608 | tf_op jit(solution)/shard_map/all_to_all | solution.py:103
  572.4 5.6 copy-start.1
Sparse Core Ops, SparseCore 0:
  207.3 283.4 all-reduce.2
where the time goes:
time: 595 us; the launch traced here: 585 us
  waiting for transfers between devices  311 us (52%)
  local copies, waits for them, and re-layouts  110 us (18%)
  starting transfers between devices  78.9 us (13%)
  matrix products  43.6 us (7%)
  other arithmetic  26.6 us (4%)
  between operations  14.9 us (3%)
    psum x1, waiting for transfers between devices, per_device(): lax.psum((part_hot, part_warm, part_cold), ('wide', 'narrow'))  184 us
    all_to_all x1, waiting for transfers between devices, per_device(): lax.all_to_all(sent_hot, 'wide', split_axis=0, concat_axis=0, tiled=True)  87.6 us
    scatter x3, local copies, waits for them, and re-layouts, pack_rows(): jnp.zeros((devices * capacity, columns), values.dtype).at[placed]  25.4 us
    scatter x3, local copies, waits for them, and re-layouts, pack_rows(): jnp.full((devices * capacity,), -1, jnp.int32).at[placed].set(local_rows)  24.7 us
    dot_general x5, matrix products, one_block(): return jnp.dot(onehot, terms, preferred_element_type=jnp.float32)  13.7 us
    dot_general x8, matrix products, one_block(): lax.dot_general(terms, onehot, (((0,), (0,)), ((), ())), preferred_elemen...  13.6 us
    all_to_all x1, starting transfers between devices, per_device(): lax.all_to_all(label_hot, 'wide', split_axis=0, concat_axis=0, tiled=True)  12 us
  transfers between devices with their start and end apart: 13, of which 8 were waited for; matrix products, arithmetic and copies ran while one was open for 24% of the time, Pallas kernels for 0%

commit v1 on v0

--- a/solution.py
+++ b/solution.py
@@ -11,6 +11,11 @@
 ROWS_HOT = 512
 ROWS_WARM = 2048
 ROWS_COLD = 4096
+
+
+def one_after_other(value, axis_one, axis_two):
+    partial = lax.psum(value, axis_one)
+    return lax.psum(partial, axis_two)
 
 
 def project(values, weight):
@@ -157,8 +162,8 @@
     )
     part_cold = jnp.dot(saved_cold, upstream_cold, preferred_element_type=jnp.float32)
     factor = 1.0 / math.sqrt(LOOK * devices)
-    total_hot, total_warm, total_cold = lax.psum(
-        (part_hot, part_warm, part_cold), ("wide", "narrow")
+    total_hot, total_warm, total_cold = one_after_other(
+        (part_hot, part_warm, part_cold), "wide", "narrow"
     )
     return (
         table_hot,

time: 595 us -> 523 us (0.88)
  waiting for transfers between devices: 311 us -> 233 us
    psum x1 -> x2, waiting for transfers between devices: 184 us -> 112 us  [the longest x1 69.9 us: one_after_other(): partial = lax.psum(value, axis_one)]
    all_to_all x1, waiting for transfers between devices: 10.2 us -> 0.01 us  [per_device(): lax.all_to_all(lax.all_to_all(sent_hot, 'wide', split_axis=0, concat_axis...]
  transfers between devices with their start and end apart: 13 -> 14, of which waited for: 8 -> 8; matrix products, arithmetic and copies ran while one was open for 24% -> 28% of each run, Pallas kernels for 0% -> 0%
where the time goes in v1:
time: 523 us; the launch traced here: 513 us
  waiting for transfers between devices  233 us (45%)
  local copies, waits for them, and re-layouts  110 us (21%)
  starting transfers between devices  84.7 us (16%)
  matrix products  43.6 us (8%)
  other arithmetic  26.1 us (5%)
  between operations  14.9 us (3%)
    all_to_all x1, waiting for transfers between devices, per_device(): lax.all_to_all(sent_hot, 'wide', split_axis=0, concat_axis=0, tiled=True)  92.3 us
    psum x1, waiting for transfers between devices, one_after_other(): partial = lax.psum(value, axis_one)  69.9 us
    psum x1, waiting for transfers between devices, one_after_other(): return lax.psum(partial, axis_two)  42 us
    scatter x3, local copies, waits for them, and re-layouts, pack_rows(): jnp.zeros((devices * capacity, columns), values.dtype).at[placed]  25.4 us
    scatter x3, local copies, waits for them, and re-layouts, pack_rows(): jnp.full((devices * capacity,), -1, jnp.int32).at[placed].set(local_rows)  24.7 us
    dot_general x5, matrix products, one_block(): return jnp.dot(onehot, terms, preferred_element_type=jnp.float32)  13.7 us
    dot_general x8, matrix products, one_block(): lax.dot_general(terms, onehot, (((0,), (0,)), ((), ())), preferred_elemen...  13.6 us
    all_to_all x1, starting transfers between devices, per_device(): lax.all_to_all(label_hot, 'wide', split_axis=0, concat_axis=0, tiled=True)  12 us
  transfers between devices with their start and end apart: 14, of which 8 were waited for; matrix products, arithmetic and copies ran while one was open for 28% of the time, Pallas kernels for 0%

profile of v1, /device:TPU:1, one launch (start us, length us, event | category | flops | bytes accessed | tf_op | source)
XLA Modules:
  0.0 512.7 jit_solution(8167377467799768238)
XLA Ops:
  8.5 1.3 copy-done.2
  9.9 1.8 broadcast_add_fusion.2
  11.7 1.2 copy.50
  14.5 8.2 %scatter_custom_fusion = s32[4096]{0:T(1024)S(1)} fusion(s32[2048]{0:T(1024)S(1)} %bitcast.108, s32[2048]{0:T(1024)} %param.31, s32[]{:T(128)} %constant.28.clone.1), kind=kCustom, calls=%fused_computation.69 | custom fusion | bytes 16896 | tf_op jit(solution)/shard_map/scatter | solution.py:34
  23.5 12.0 %all-to-all-start = ((s32[32,1,128]{2,1,0:T(1,128)}), s32[32,1,128]{2,1,0:T(1,128)S(1)}, u32[]{:S(2)}, u32[]{:S(2)}) async-start(s32[32,1,128]{2,1,0:T(1,128)} %reshape.208), calls=%async_computation | async-start | bytes 32768 | tf_op jit(solution)/shard_map/all_to_all | solution.py:130
  36.0 1.3 copy-done.3
  37.4 1.8 broadcast_add_fusion.1
  41.9 1.3 copy-done.4
  43.3 1.8 broadcast_add_fusion
  47.3 8.2 %scatter_custom_fusion.2 = s32[4096]{0:T(1024)S(1)} fusion(s32[2048]{0:T(1024)S(1)} %bitcast.110, s32[2048]{0:T(1024)} %param.32, s32[]{:T(128)} %constant.28.clone.1), kind=kCustom, calls=%fused_computation.67 | custom fusion | bytes 16896 | tf_op jit(solution)/shard_map/scatter | solution.py:34
  56.3 9.2 %all-to-all-start.4 = ((s32[32,1,128]{2,1,0:T(1,128)}), s32[32,1,128]{2,1,0:T(1,128)S(1)}, u32[]{:S(2)}, u32[]{:S(2)}) async-start(s32[32,1,128]{2,1,0:T(1,128)} %reshape.212), calls=%async_computation.4 | async-start | bytes 32768 | tf_op jit(solution)/shard_map/all_to_all | solution.py:137
  65.6 8.2 %scatter_custom_fusion.4 = s32[4096]{0:T(1024)S(1)} fusion(s32[2048]{0:T(1024)S(1)} %bitcast.112, s32[2048]{0:T(1024)} %param.33, s32[]{:T(128)} %constant.28.clone.1), kind=kCustom, calls=%fused_computation.65 | custom fusion | bytes 16896 | tf_op jit(solution)/shard_map/scatter | solution.py:34
  74.6 9.2 %all-to-all-start.8 = ((s32[32,1,128]{2,1,0:T(1,128)}), s32[32,1,128]{2,1,0:T(1,128)S(1)}, u32[]{:S(2)}, u32[]{:S(2)}) async-start(s32[32,1,128]{2,1,0:T(1,128)} %reshape.216), calls=%async_computation.8 | async-start | bytes 32768 | tf_op jit(solution)/shard_map/all_to_all | solution.py:144
  85.9 6.5 %all-to-all-done.8 = s32[32,1,128]{2,1,0:T(1,128)S(1)} async-done(((s32[32,1,128]{2,1,0:T(1,128)}), s32[32,1,128]{2,1,0:T(1,128)S(1)}, u32[]{:S(2)}, u32[]{:S(2)}) %all-to-all-start.8) | async-done | bytes 16416 | tf_op jit(solution)/shard_map/all_to_all | solution.py:144
  92.4 7.5 %all-to-all-start.1 = ((s32[8,1,512]{2,1,0:T(1,128)}), s32[8,1,512]{2,1,0:T(1,128)S(1)}, u32[]{:S(2)}, u32[]{:S(2)}) async-start(s32[8,1,512]{2,1,0:T(1,128)} %reshape.210), calls=%async_computation.1 | async-start | bytes 32768 | tf_op jit(solution)/shard_map/all_to_all | solution.py:129
  101.4 3.1 all-to-all-done.1
  104.6 3.9 all-to-all-start.5
  108.5 2.3 convolution_convert_fusion.2
  111.9 6.4 %scatter_custom_fusion.5 = bf16[4096,32]{1,0:T(8,128)(2,1)S(1)} fusion(s32[2048]{0:T(1024)S(1)} %bitcast.113, bf16[2048,32]{1,0:T(8,128)(2,1)} %copy.64, bf16[]{:T(256)} %constant.37.clone.1), kind=kCustom, calls=%fused_computation.53 | custom fusion | bytes 262656 | tf_op jit(solution)/shard_map/scatter | solution.py:33
  118.3 1.7 reshape.145
  120.0 3.9 all-to-all-start.10
  125.4 10.6 %all-to-all-done.10 = bf16[32,8,512]{2,1,0:T(8,128)(2,1)S(1)} async-done(((bf16[32,8,512]{2,1,0:T(8,128)(2,1)}), bf16[32,8,512]{2,1,0:T(8,128)(2,1)S(1)}, u32[]{:S(2)}, u32[]{:S(2)}) %all-to-all-start.10) | async-done | bytes 262176 | tf_op jit(solution)/shard_map/all_to_all | solution.py:123
  136.0 6.2 %all-to-all-start.9 = ((s32[8,1,512]{2,1,0:T(1,128)}), s32[8,1,512]{2,1,0:T(1,128)S(1)}, u32[]{:S(2)}, u32[]{:S(2)}) async-start(s32[8,1,512]{2,1,0:T(1,128)} %reshape.218), calls=%async_computation.9 | async-start | bytes 32768 | tf_op jit(solution)/shard_map/all_to_all | solution.py:143
  143.0 3.9 all-to-all-done.9
  147.4 4.0 all-to-all-start.11
  151.5 3.1 convolution_convert_fusion.1
  154.6 6.4 %scatter_custom_fusion.3 = bf16[4096,128]{1,0:T(8,128)(2,1)S(1)} fusion(s32[2048]{0:T(1024)} %bitcast.111, bf16[2048,128]{1,0:T(8,128)(2,1)} %convolution_convert_fusion.1, bf16[]{:T(256)} %constant.37.clone.1), kind=kCustom, calls=%fused_computation.55 | custom fusion | bytes 1049088 | tf_op jit(solution)/shard_map/scatter | solution.py:33
  161.0 1.3 reshape.140
  162.3 4.1 all-to-all-start.6
  166.4 3.7 convolution_convert_fusion
  170.0 12.6 %scatter_custom_fusion.1 = bf16[4096,512]{1,0:T(8,128)(2,1)} fusion(s32[2048]{0:T(1024)} %bitcast.109, bf16[2048,512]{1,0:T(8,128)(2,1)} %convolution_convert_fusion, bf16[]{:T(256)} %constant.37.clone.1), kind=kCustom, calls=%fused_computation.40 | custom fusion | bytes 4194816 | tf_op jit(solution)/shard_map/scatter | solution.py:33
  182.6 7.4 %reshape.136 = bf16[32,8,8192]{2,1,0:T(8,128)(2,1)} reshape(bf16[4096,512]{1,0:T(8,128)(2,1)} %scatter_custom_fusion.1) | data formatting | bytes 8388608 | tf_op jit(solution)/shard_map/reshape | solution.py:37
  190.0 4.4 all-to-all-done.6
  194.4 5.3 %all-to-all-start.2 = ((bf16[32,8,8192]{2,1,0:T(8,128)(2,1)}), bf16[32,8,8192]{2,1,0:T(8,128)(2,1)}, u32[]{:S(2)}, u32[]{:S(2)}) async-start(bf16[32,8,8192]{2,1,0:T(8,128)(2,1)} %reshape.136), calls=%async_computation.2 | async-start | bytes 8388608 | tf_op jit(solution)/shard_map/all_to_all | solution.py:109
  199.8 2.8 fusion.48
  202.6 2.2 fusion.47
  204.9 2.2 fusion.46
  207.2 1.5 copy.58
  208.7 92.3 %all-to-all-done.2 = bf16[32,8,8192]{2,1,0:T(8,128)(2,1)} async-done(((bf16[32,8,8192]{2,1,0:T(8,128)(2,1)}), bf16[32,8,8192]{2,1,0:T(8,128)(2,1)}, u32[]{:S(2)}, u32[]{:S(2)}) %all-to-all-start.2) | async-done | bytes 4194336 | tf_op jit(solution)/shard_map/all_to_all | solution.py:109
  301.0 9.0 %all-to-all-start.7 = ((bf16[32,8,2048]{2,0,1:T(8,128)(2,1)}), bf16[32,8,2048]{2,0,1:T(8,128)(2,1)S(1)}, u32[]{:S(2)}, u32[]{:S(2)}) async-start(bf16[32,8,2048]{2,0,1:T(8,128)(2,1)} %copy.58), calls=%async_computation.7 | async-start | bytes 2097152 | tf_op jit(solution)/shard_map/all_to_all | solution.py:115
  313.6 69.9 %all-reduce.5.cloned.1.call-done = (f32[512,512]{1,0:T(8,128)}, f32[128,512]{1,0:T(8,128)}, f32[32,512]{1,0:T(8,128)}) async-done(((f32[512,512]{1,0:T(8,128)}, f32[128,512]{1,0:T(8,128)}, f32[32,512]{1,0:T(8,128)}), (f32[512,512]{1,0:T(8,128)}, f32[128,512]{1,0:T(8,128)}, f32[32,512]{1,0:T(8,128)})) %all-reduce.5.cloned.1.call-update) | async-done | bytes 1376272 | tf_op jit(solution)/shard_map/psum | solution.py:17
  383.5 6.5 %copy.53 = bf16[32,8,8192]{2,0,1:T(8,128)(2,1)} copy(bf16[32,8,8192]{2,1,0:T(8,128)(2,1)} %all-to-all-done.2) | data formatting | bytes 8388608 | tf_op jit(solution)/shard_map/all_to_all | solution.py:109
  390.0 10.2 %all-to-all-start.3 = ((bf16[32,8,8192]{2,0,1:T(8,128)(2,1)}), bf16[32,8,8192]{2,0,1:T(8,128)(2,1)}, u32[]{:S(2)}, u32[]{:S(2)}) async-start(bf16[32,8,8192]{2,0,1:T(8,128)(2,1)} %copy.53), calls=%async_computation.3 | async-start | bytes 8388608 | tf_op jit(solution)/shard_map/all_to_all | solution.py:108
  400.1 23.5 %while.27 = (s32[]{:T(128)}, f32[8,32,512]{2,1,0:T(8,128)S(1)}, s32[32,8,16]{2,1,0:T(8,128)}, s32[8]{0:T(128)S(1)}, bf16[4096,32]{1,0:T(8,128)(2,1)S(1)}, /*index=5*/s32[4096]{0:T(1024)S(1)}, s32[]{:T(128)}) while((s32[]{:T(128)}, f32[8,32,512]{2,1,0:T(8,128)S(1)}, s32[32,8,16]{2,1,0:T(8,128)}, s32[8]{0:T(128)S(1)}, ...), condition=%wide.wide.region_18.19_spmd, body=%wide.wide.region_17.18_spmd.sunk | while | flops 136315392 | bytes 1134697 | solution.py:57
  401.4 1.7 fusion.81
  404.3 1.7 fusion.81
  407.3 1.7 fusion.81
  410.2 1.7 fusion.81
  413.2 1.7 fusion.81
  416.1 1.7 fusion.81
  419.0 1.7 fusion.81
  422.0 1.7 fusion.81
  424.5 42.0 %all-reduce.7.cloned.1.call-done = (f32[512,512]{1,0:T(8,128)}, f32[128,512]{1,0:T(8,128)}, f32[32,512]{1,0:T(8,128)}) async-done(((f32[512,512]{1,0:T(8,128)}, f32[128,512]{1,0:T(8,128)}, f32[32,512]{1,0:T(8,128)}), (f32[512,512]{1,0:T(8,128)}, f32[128,512]{1,0:T(8,128)}, f32[32,512]{1,0:T(8,128)})) %all-reduce.7.cloned.1.call-update) | async-done | bytes 1376272 | tf_op jit(solution)/shard_map/psum | solution.py:18
  466.5 1.5 broadcast_multiply_fusion.2
  468.0 1.7 broadcast_multiply_fusion.1
  469.7 2.3 broadcast_multiply_fusion
  473.1 13.0 %while.26 = (s32[]{:T(128)}, f32[4,512,128]{2,1,0:T(8,128)}, s32[4]{0:T(128)S(1)}, s32[32,8,16]{2,1,0:T(8,128)}, bf16[4096,128]{1,0:T(8,128)(2,1)S(1)}, /*index=5*/s32[4096]{0:T(1024)S(1)}, s32[]{:T(128)}) while((s32[]{:T(128)}, f32[4,512,128]{2,1,0:T(8,128)}, s32[4]{0:T(128)S(1)}, s32[32,8,16]{2,1,0:T(8,128)}, ...), condition=%wide.wide.region_11.12_spmd, body=%wide.wide.region_10.11_spmd.sunk | while | flops 538968576 | bytes 1331305 | solution.py:57
  474.3 2.0 fusion.78
  477.6 2.0 fusion.78
  480.8 2.0 fusion.78
  484.1 2.0 fusion.78
  486.1 6.5 %copy.54 = bf16[32,8,8192]{2,1,0:T(8,128)(2,1)} copy(bf16[32,8,8192]{2,0,1:T(8,128)(2,1)} %all-to-all-done.3) | data formatting | bytes 8388608 | tf_op jit(solution)/shard_map/all_to_all | solution.py:108
  492.5 7.4 %reshape.137 = bf16[4096,512]{1,0:T(8,128)(2,1)} reshape(bf16[32,8,8192]{2,1,0:T(8,128)(2,1)} %copy.54) | data formatting | bytes 8388608 | tf_op jit(solution)/shard_map/reshape | solution.py:151
  499.9 5.6 %fusion.20 = f32[512,512]{1,0:T(8,128)} fusion(bf16[4096,512]{1,0:T(8,128)(2,1)} %reshape.137, s32[4096]{0:T(1024)S(1)} %eq.136), kind=kOutput, calls=%fused_computation.21 | convolution fusion | flops 2149580800 | bytes 5259264 | tf_op jit(solution)/shard_map/while/body/eval_jaxpr/dot_general | solution.py:54
  (141 shorter events, 38.2 us)
Async XLA Ops:
  7.2 159.2 %copy-start = (bf16[2048,512]{1,0:T(8,128)(2,1)S(1)}, bf16[2048,512]{1,0:T(8,128)(2,1)}, u32[]{:S(2)}) copy-start(bf16[2048,512]{1,0:T(8,128)(2,1)} %param.19) | copy-start | bytes 6291460
  8.5 1.4 copy-start.2
  11.7 1.3 copy-start.10
  12.9 22.6 %copy-start.11 = (s32[2048,1]{0,1:T(1,128)S(1)}, s32[2048,1]{0,1:T(1,128)}, u32[]{:S(2)}) copy-start(s32[2048,1]{0,1:T(1,128)} %param.29) | copy-start | bytes 24580
  13.9 0.6 copy-start.18
  23.5 32.8 %all-to-all-start = ((s32[32,1,128]{2,1,0:T(1,128)}), s32[32,1,128]{2,1,0:T(1,128)S(1)}, u32[]{:S(2)}, u32[]{:S(2)}) async-start(s32[32,1,128]{2,1,0:T(1,128)} %reshape.208), calls=%async_computation | async-start | bytes 32768 | tf_op jit(solution)/shard_map/all_to_all | solution.py:130
  36.0 1.4 copy-start.3
  40.5 1.0 copy-start.12
  41.4 5.8 %copy-start.19 = (s32[2048,1]{0,1:T(1,128)}, s32[2048,1]{0,1:T(1,128)S(1)}, u32[]{:S(2)}) copy-start(s32[2048,1]{0,1:T(1,128)S(1)} %compare_select_fusion.1) | copy-start | bytes 24580
  41.9 1.4 copy-start.4
  46.3 62.2 %copy-start.17 = (bf16[32,512]{1,0:T(8,128)(2,1)S(1)}, bf16[32,512]{1,0:T(8,128)(2,1)}, u32[]{:S(2)}) copy-start(bf16[32,512]{1,0:T(8,128)(2,1)} %param.27) | copy-start | bytes 98308
  56.3 18.3 %all-to-all-start.4 = ((s32[32,1,128]{2,1,0:T(1,128)}), s32[32,1,128]{2,1,0:T(1,128)S(1)}, u32[]{:S(2)}, u32[]{:S(2)}) async-start(s32[32,1,128]{2,1,0:T(1,128)} %reshape.212), calls=%async_computation.4 | async-start | bytes 32768 | tf_op jit(solution)/shard_map/all_to_all | solution.py:137
  74.6 17.8 %all-to-all-start.8 = ((s32[32,1,128]{2,1,0:T(1,128)}), s32[32,1,128]{2,1,0:T(1,128)S(1)}, u32[]{:S(2)}, u32[]{:S(2)}) async-start(s32[32,1,128]{2,1,0:T(1,128)} %reshape.216), calls=%async_computation.8 | async-start | bytes 32768 | tf_op jit(solution)/shard_map/all_to_all | solution.py:144
  92.4 12.2 %all-to-all-start.1 = ((s32[8,1,512]{2,1,0:T(1,128)}), s32[8,1,512]{2,1,0:T(1,128)S(1)}, u32[]{:S(2)}, u32[]{:S(2)}) async-start(s32[8,1,512]{2,1,0:T(1,128)} %reshape.210), calls=%async_computation.1 | async-start | bytes 32768 | tf_op jit(solution)/shard_map/all_to_all | solution.py:129
  104.6 15.4 %all-to-all-start.5 = ((s32[8,1,512]{2,1,0:T(1,128)}), s32[8,1,512]{2,1,0:T(1,128)S(1)}, u32[]{:S(2)}, u32[]{:S(2)}) async-start(s32[8,1,512]{2,1,0:T(1,128)} %reshape.214), calls=%async_computation.5 | async-start | bytes 32768 | tf_op jit(solution)/shard_map/all_to_all | solution.py:136
  111.9 39.6 %copy-start.9 = (bf16[128,512]{1,0:T(8,128)(2,1)S(1)}, bf16[128,512]{1,0:T(8,128)(2,1)}, u32[]{:S(2)}) copy-start(bf16[128,512]{1,0:T(8,128)(2,1)} %param.26) | copy-start | bytes 393220
  120.0 26.9 %copy-start.13 = (s32[8,1,512]{2,1,0:T(1,128)}, s32[8,1,512]{2,1,0:T(1,128)S(1)}, u32[]{:S(2)}) copy-start(s32[8,1,512]{2,1,0:T(1,128)S(1)} %all-to-all-done.5) | copy-start | bytes 49156
  120.0 16.0 %all-to-all-start.10 = ((bf16[32,8,512]{2,1,0:T(8,128)(2,1)}), bf16[32,8,512]{2,1,0:T(8,128)(2,1)S(1)}, u32[]{:S(2)}, u32[]{:S(2)}) async-start(bf16[32,8,512]{2,1,0:T(8,128)(2,1)} %reshape.145), calls=%async_computation.10 | async-start | bytes 524288 | tf_op jit(solution)/shard_map/all_to_all | solution.py:123
  136.0 10.9 %all-to-all-start.9 = ((s32[8,1,512]{2,1,0:T(1,128)}), s32[8,1,512]{2,1,0:T(1,128)S(1)}, u32[]{:S(2)}, u32[]{:S(2)}) async-start(s32[8,1,512]{2,1,0:T(1,128)} %reshape.218), calls=%async_computation.9 | async-start | bytes 32768 | tf_op jit(solution)/shard_map/all_to_all | solution.py:143
  146.8 0.6 copy-start.15
  147.4 14.8 %all-to-all-start.11 = ((bf16[32,8,512]{2,0,1:T(8,128)(2,1)}), bf16[32,8,512]{2,0,1:T(8,128)(2,1)S(1)}, u32[]{:S(2)}, u32[]{:S(2)}) async-start(bf16[32,8,512]{2,0,1:T(8,128)(2,1)} %copy.65), calls=%async_computation.11 | async-start | bytes 524288 | tf_op jit(solution)/shard_map/all_to_all | solution.py:122
  162.3 32.2 %all-to-all-start.6 = ((bf16[32,8,2048]{2,1,0:T(8,128)(2,1)}), bf16[32,8,2048]{2,1,0:T(8,128)(2,1)S(1)}, u32[]{:S(2)}, u32[]{:S(2)}) async-start(bf16[32,8,2048]{2,1,0:T(8,128)(2,1)} %reshape.140), calls=%async_computation.6 | async-start | bytes 2097152 | tf_op jit(solution)/shard_map/all_to_all | solution.py:116
  190.0 9.8 %copy-start.8 = (bf16[32,2048]{1,0:T(8,128)(2,1)S(1)}, bf16[32,2048]{1,0:T(8,128)(2,1)}, u32[]{:S(2)}) copy-start(bf16[32,2048]{1,0:T(8,128)(2,1)} %param.24) | copy-start | bytes 393220
  194.4 106.6 %all-to-all-start.2 = ((bf16[32,8,8192]{2,1,0:T(8,128)(2,1)}), bf16[32,8,8192]{2,1,0:T(8,128)(2,1)}, u32[]{:S(2)}, u32[]{:S(2)}) async-start(bf16[32,8,8192]{2,1,0:T(8,128)(2,1)} %reshape.136), calls=%async_computation.2 | async-start | bytes 8388608 | tf_op jit(solution)/shard_map/all_to_all | solution.py:109
  199.7 183.8 %all-reduce.5.cloned.1.call-start = ((), (), s32[]{:S(2)}) async-start(), calls=%async_computation.12 | async-start | bytes 2752512 | tf_op jit(solution)/shard_map/psum | solution.py:17
  199.8 2.9 copy-start.5
  199.8 5.1 copy-start.20
  207.1 103.9 %copy-start.14 = (s32[8,1,512]{2,1,0:T(1,128)S(1)}, s32[8,1,512]{2,1,0:T(1,128)}, u32[]{:S(2)}) copy-start(s32[8,1,512]{2,1,0:T(1,128)} %copy-done.13) | copy-start | bytes 49156
  207.1 104.8 %copy-start.16 = (s32[8,1,512]{2,1,0:T(1,128)S(1)}, s32[8,1,512]{2,1,0:T(1,128)}, u32[]{:S(2)}) copy-start(s32[8,1,512]{2,1,0:T(1,128)} %copy-done.15) | copy-start | bytes 49156
  301.0 89.0 %all-to-all-start.7 = ((bf16[32,8,2048]{2,0,1:T(8,128)(2,1)}), bf16[32,8,2048]{2,0,1:T(8,128)(2,1)S(1)}, u32[]{:S(2)}, u32[]{:S(2)}) async-start(bf16[32,8,2048]{2,0,1:T(8,128)(2,1)} %copy.58), calls=%async_computation.7 | async-start | bytes 2097152 | tf_op jit(solution)/shard_map/all_to_all | solution.py:115
  310.1 156.4 %all-reduce.7.cloned.1.call-start = ((), (), s32[]{:S(2)}) async-start(), calls=%async_computation.13 | async-start | bytes 2752512 | tf_op jit(solution)/shard_map/psum | solution.py:18
  311.8 78.2 %copy-start.6 = (s32[32,8,16]{2,1,0:T(8,128)}, s32[32,8,16]{2,1,0:T(8,128)S(1)}, u32[]{:S(2)}) copy-start(s32[32,8,16]{2,1,0:T(8,128)S(1)} %copy.60) | copy-start | bytes 49156
  312.7 77.2 %copy-start.7 = (s32[32,8,16]{2,1,0:T(8,128)}, s32[32,8,16]{2,1,0:T(8,128)S(1)}, u32[]{:S(2)}) copy-start(s32[32,8,16]{2,1,0:T(8,128)S(1)} %copy.67) | copy-start | bytes 49156
  390.0 96.1 %all-to-all-start.3 = ((bf16[32,8,8192]{2,0,1:T(8,128)(2,1)}), bf16[32,8,8192]{2,0,1:T(8,128)(2,1)}, u32[]{:S(2)}, u32[]{:S(2)}) async-start(bf16[32,8,8192]{2,0,1:T(8,128)(2,1)} %copy.53), calls=%async_computation.3 | async-start | bytes 8388608 | tf_op jit(solution)/shard_map/all_to_all | solution.py:108
  499.9 5.6 %copy-start.1 = (bf16[2048,512]{1,0:T(8,128)(2,1)S(1)}, bf16[2048,512]{1,0:T(8,128)(2,1)}, u32[]{:S(2)}) copy-start(bf16[2048,512]{1,0:T(8,128)(2,1)} %param.19) | copy-start | bytes 6291460
Sparse Core Ops, SparseCore 0:
  207.3 176.1 all-reduce.4
  386.0 80.4 all-reduce.6
